TPU v7x, 512 devices: a whole 4x8x8 slice. The times are simulated.
512 devices in a mesh: gz: 8 (over x, z_lo), row: 8 (over z_hi, core), col: 8 (over y).
Axes of the slice: x: 4, y: 8, z: 8 (z_hi: 4, z_lo: 2; z = z_hi * 2 + z_lo), core: 2. Of those that a mesh axis runs over, the one named last changes fastest.
Arguments:
- front: float32 [4096, 4096], P('row', 'col'), may hold values from -0.04 to 1.45
- lower_parts: float32 [8, 4096, 256], P('gz', 'row'), may hold values from -0.1875 to 0.1875
- upper_parts: float32 [8, 256, 4096], P('gz', None, 'col'), may hold values from -0.125 to 0.125
- pattern: int32 [8, 32, 2], P('gz', 'row'), may hold values 0 or 1
- row_perm: int32 [8, 512], P('row'), may hold values from 0 to 511, as said below
Outputs:
- factored: float32 [4096, 4096], P('row', 'col')
Inputs may be any that keep to these rules, and one draw needn't show every extreme that they name: `row_perm`: each of the 8 rows holds every number 0 to 511 once.
All inputs are finite; a program needn't handle non-finite values. No bound on the sum of `pattern` on one device may be relied on, other than what follows from the above.
Results may differ from a plain program's by a relative error of at most 0.0001.
Values sent between devices are 32-bit elements; how exact they have to be, the bound alone decides.
A program may use at most 64 MiB of HBM per device.

v0:
```python
import jax
import jax.numpy as jnp
from jax import lax
from jax.sharding import PartitionSpec as P

BS = 128
NS_STEPS = 3
PANELS = 2
precise = lax.Precision.HIGHEST


def spread(value, axis, root):
    mine = lax.axis_index(axis) == root
    return lax.psum(jnp.where(mine, value, jnp.zeros_like(value)), axis)


def product(first_matrix, second_matrix):
    return jnp.dot(
        first_matrix, second_matrix, precision=precise, preferred_element_type=jnp.float32
    )


def advance_rows(own_rows, pivot_block, full_inverse):
    return 2.0 * own_rows - product(product(own_rows, pivot_block), full_inverse)


def newton_inverse(pivot_block):
    block_width = pivot_block.shape[0]
    full_inverse = 2.0 * jnp.eye(block_width, dtype=jnp.float32) - pivot_block
    for iteration in range(NS_STEPS - 1):
        full_inverse = advance_rows(full_inverse, pivot_block, full_inverse)
    return full_inverse


def on_device(front, lower_parts, upper_parts, pattern, row_perm):
    panel_width = row_perm.shape[1]
    local_rows, local_cols = front.shape
    blocks_down = local_rows // panel_width
    blocks_across = local_cols // panel_width
    inner_cols = lower_parts.shape[2]
    masked = lower_parts[0].reshape(local_rows // BS, BS, inner_cols // BS, BS)
    masked = masked * pattern[0].astype(jnp.float32)[:, None, :, None]
    partial_value = product(masked.reshape(local_rows, inner_cols), upper_parts[0])
    merged = front - lax.psum(partial_value, "gz")
    sources = (jnp.arange(blocks_down, dtype=jnp.int32) * panel_width)[:, None] + row_perm
    factored = jnp.take(merged, sources.reshape(local_rows), axis=0)
    grid_row = lax.axis_index("row")
    grid_col = lax.axis_index("col")
    row_panels = grid_row * blocks_down + jnp.arange(local_rows, dtype=jnp.int32) // panel_width
    col_panels = grid_col * blocks_across + jnp.arange(local_cols, dtype=jnp.int32) // panel_width
    identity = jnp.eye(panel_width, dtype=jnp.float32)
    for panel_index in range(PANELS):
        owner_row = panel_index // blocks_down
        owner_col = panel_index // blocks_across
        row_start = panel_index % blocks_down * panel_width
        col_start = panel_index % blocks_across * panel_width
        panel_row = spread(factored, "row", owner_row)
        in_column = grid_col == owner_col
        pivot_block = jnp.where(in_column, panel_row, identity)
        inverse = newton_inverse(pivot_block)
        column_block = factored
        lower_own = product(column_block, inverse)
        lower_recv = spread(lower_own, "col", owner_col)
        below_rows = row_panels > panel_index
        trailing = below_rows[:, None] & (col_panels > panel_index)[None, :]
        factored = factored - jnp.where(trailing, product(lower_recv, panel_row), 0.0)
        current = factored
        stacked = jnp.tile(inverse, (blocks_down, 1))
        diagonal_rows = row_panels == panel_index
        replaced = jnp.where(
            below_rows[:, None], lower_own, jnp.where(diagonal_rows[:, None], stacked, current)
        )
        factored = factored.at[:, col_start : col_start + panel_width].set(
            jnp.where(in_column, replaced, current)
        )
    return factored


def solution(mesh):
    in_specs = (
        P("row", "col"),
        P("gz", "row", None),
        P("gz", None, "col"),
        P("gz", "row", None),
        P("row", None),
    )
    out_specs = P("row", "col")
    return jax.shard_map(
        on_device, mesh=mesh, in_specs=in_specs, out_specs=out_specs, check_vma=False
    )
```

profile of v0, /device:TPU:2, one launch (start us, length us, event | category | flops | bytes accessed | tf_op | source)
XLA Modules:
  0.0 472.1 jit_solution(3480206786806552087)
XLA Ops:
  6.5 0.0 copy-start
  6.5 0.0 all-reduce.6.cloned.1.call-start
  6.5 0.7 convert_bitcast_fusion
  7.3 0.1 copy.7
  7.4 0.2 mul.32
  7.6 0.0 copy-start.6
  7.6 0.4 mul.33
  8.0 0.0 copy-done
  8.0 0.6 copy-done.6
  8.6 2.0 fusion.10
  10.6 0.0 copy-start.5
  10.6 0.0 all-reduce.6.cloned.1.call-update
  10.7 0.0 all-reduce.8.cloned.1.call-start
  10.7 0.0 copy-start.7
  10.7 0.7 copy-done.7
  11.5 92.9 %all-reduce.6.cloned.1.call-done = f32[512,512]{1,0:T(8,128)} async-done(((f32[512,512]{1,0:T(8,128)}), f32[512,512]{1,0:T(8,128)}) %all-reduce.6.cloned.1.call-update) | async-done | bytes 1048592 | tf_op jit(solution)/shard_map/psum | solution.py:44
  104.4 0.0 copy-done.5
  104.4 1.4 sub.38
  105.9 1.6 gather_fusion
  107.5 1.1 select_select_fusion.2
  108.6 0.0 all-reduce.8.cloned.1.call-update
  108.7 0.0 all-reduce.10.cloned.1.call-start
  108.7 83.7 %all-reduce.8.cloned.1.call-done = f32[512,512]{1,0:T(8,128)} async-done(((f32[512,512]{1,0:T(8,128)}), f32[512,512]{1,0:T(8,128)}) %all-reduce.8.cloned.1.call-update) | async-done | bytes 1048592 | tf_op jit(solution)/shard_map/psum | solution.py:14
  192.4 0.0 copy-start.1
  192.4 3.6 fusion.2
  196.0 0.0 copy-done.1
  196.0 1.9 convolution_subtract_fusion.3
  197.9 1.9 fusion.8
  199.8 1.9 convolution_subtract_fusion.2
  201.7 0.0 copy-start.3
  201.7 3.2 broadcast_select_fusion.2
  204.9 0.0 copy-done.3
  204.9 0.0 all-reduce.10.cloned.1.call-update
  205.0 0.2 all-reduce.12.cloned.1.call-start
  205.2 77.8 %all-reduce.10.cloned.1.call-done = f32[512,512]{1,0:T(8,128)} async-done(((f32[512,512]{1,0:T(8,128)}), f32[512,512]{1,0:T(8,128)}) %all-reduce.10.cloned.1.call-update) | async-done | bytes 1048592 | tf_op jit(solution)/shard_map/psum | solution.py:14
  283.0 5.2 %broadcast_select_fusion.1 = (f32[512,512]{1,0:T(8,128)}, f32[512,512]{1,0:T(8,128)}) fusion(pred[]{:T(512)S(6)} %eq.44, f32[512,512]{1,0:T(8,128)} %get-tuple-element.46, f32[512,512]{1,0:T(8,128)} %copy-done.3, f32[512,512]{1,0:T(8,128)} %all-reduce.10.cloned.1.call-done, f32[512,512]{1,0:T(8,128)S(1)} %copy-done.1, pred[512]{0:T(512)(128)(4,1)S(1)} %fusion.36, ...), kind=kOutput, calls=%fused_computation.32 | convolution fusion | flops 1612709888 | bytes 7342082 | tf_op jit(solution)/shard_map/dot_general | solution.py:18
  288.3 0.0 all-reduce.12.cloned.1.call-update
  288.3 0.0 all-reduce.14.cloned.1.call-start
  288.3 81.9 %all-reduce.12.cloned.1.call-done = f32[512,512]{1,0:T(8,128)} async-done(((f32[512,512]{1,0:T(8,128)}), f32[512,512]{1,0:T(8,128)}) %all-reduce.12.cloned.1.call-update) | async-done | bytes 1048592 | tf_op jit(solution)/shard_map/psum | solution.py:14
  370.2 0.0 copy-start.2
  370.2 2.0 fusion.4
  372.2 0.0 copy-done.2
  372.2 1.9 convolution_subtract_fusion.1
  374.1 1.9 fusion.9
  376.0 0.0 copy-start.4
  376.0 1.8 convolution_subtract_fusion
  377.9 0.0 copy-done.4
  377.9 3.2 broadcast_select_fusion
  381.1 0.0 all-reduce.14.cloned.1.call-update
  381.1 79.7 %all-reduce.14.cloned.1.call-done = f32[512,512]{1,0:T(8,128)} async-done(((f32[512,512]{1,0:T(8,128)}), f32[512,512]{1,0:T(8,128)}) %all-reduce.14.cloned.1.call-update) | async-done | bytes 1048592 | tf_op jit(solution)/shard_map/psum | solution.py:14
  460.8 4.8 %select_select_fusion = f32[512,512]{1,0:T(8,128)} fusion(f32[512,512]{1,0:T(8,128)} %get-tuple-element.50, f32[512,512]{1,0:T(8,128)S(1)} %convolution_subtract_fusion, f32[512,512]{1,0:T(8,128)} %get-tuple-element.48, f32[512,512]{1,0:T(8,128)} %all-reduce.14.cloned.1.call-done, f32[512,512]{1,0:T(8,128)S(1)} %copy-done.2, ...), kind=kOutput, calls=%fused_computation.17 | convolution fusion | flops 1612185600 | bytes 6292993 | tf_op jit(solution)/shard_map/dot_general | solution.py:18
  (7 shorter events, 0.1 us)
Async XLA Ops:
  6.5 1.5 copy-start
  6.5 97.9 %all-reduce.6.cloned.1.call-start = ((), (), s32[]{:S(2)}) async-start(), calls=%async_computation | async-start | bytes 2097152 | tf_op jit(solution)/shard_map/psum | solution.py:44
  7.6 1.0 copy-start.6
  10.6 93.8 %copy-start.5 = (f32[512,512]{1,0:T(8,128)S(1)}, f32[512,512]{1,0:T(8,128)}, u32[]{:S(2)}) copy-start(f32[512,512]{1,0:T(8,128)} %param.13) | copy-start | bytes 3145732
  10.7 181.7 %all-reduce.8.cloned.1.call-start = ((), (), s32[]{:S(2)}) async-start(), calls=%async_computation.1 | async-start | bytes 2097152 | tf_op jit(solution)/shard_map/psum | solution.py:14
  10.7 0.8 copy-start.7
  108.7 174.4 %all-reduce.10.cloned.1.call-start = ((), (), s32[]{:S(2)}) async-start(), calls=%async_computation.2 | async-start | bytes 2097152 | tf_op jit(solution)/shard_map/psum | solution.py:14
  192.4 3.6 copy-start.1
  201.7 3.2 copy-start.3
  205.0 165.3 %all-reduce.12.cloned.1.call-start = ((), (), s32[]{:S(2)}) async-start(), calls=%async_computation.3 | async-start | bytes 2097152 | tf_op jit(solution)/shard_map/psum | solution.py:14
  288.3 172.5 %all-reduce.14.cloned.1.call-start = ((), (), s32[]{:S(2)}) async-start(), calls=%async_computation.4 | async-start | bytes 2097152 | tf_op jit(solution)/shard_map/psum | solution.py:14
  370.2 2.0 copy-start.2
  376.0 1.9 copy-start.4
Sparse Core Ops, SparseCore 0:
  10.8 93.6 all-reduce.5
  108.8 83.5 all-reduce.7
  205.1 77.9 all-reduce.9
  288.4 81.7 all-reduce.11
  381.2 79.5 all-reduce.13
where the time goes:
time: 472 us
  waiting for transfers between devices  416 us (88%)
  matrix products  35.3 us (7%)
  between operations  13.4 us (3%)
    psum x4, waiting for transfers between devices, spread(): return lax.psum(jnp.where(mine, value, jnp.zeros_like(value)), axis)  323 us
    psum x1, waiting for transfers between devices, on_device(): merged = front - lax.psum(partial_value, 'gz')  92.9 us
    dot_general x13, matrix products, product(): jnp.dot(first_matrix, second_matrix, precision=precise, preferred_element...  35.3 us
  transfers between devices with their start and end apart: 5, of which 5 were waited for; matrix products, arithmetic and copies ran while one was open for 0% of the time, Pallas kernels for 0%

commit v1 on v0

--- a/solution.py
+++ b/solution.py
@@ -11,7 +11,7 @@
 
 def spread(value, axis, root):
     mine = lax.axis_index(axis) == root
-    return lax.psum(jnp.where(mine, value, jnp.zeros_like(value)), axis)
+    return jnp.sum(lax.all_gather(jnp.where(mine, value, jnp.zeros_like(value)), axis), axis=0)
 
 
 def product(first_matrix, second_matrix):

time: 472 us -> 541 us (1.15)
  the two profiles are of different devices: /device:TPU:2 before, /device:TPU:1 now
where the time goes in v1:
time: 541 us
  waiting for transfers between devices  464 us (86%)
  matrix products  34.7 us (6%)
  other arithmetic  24.9 us (5%)
  between operations  13.3 us (2%)
    all_gather x4, waiting for transfers between devices, spread(): lax.all_gather(jnp.where(mine, value, jnp.zeros_like(value)), axis)  373 us
    psum x1, waiting for transfers between devices, on_device(): merged = front - lax.psum(partial_value, 'gz')  90.8 us
    dot_general x13, matrix products, product(): jnp.dot(first_matrix, second_matrix, precision=precise, preferred_element...  34.7 us
    reduce_sum x4, other arithmetic, spread(): jnp.sum(lax.all_gather(jnp.where(mine, value, jnp.zeros_like(value)), axi...  19.9 us
  transfers between devices with their start and end apart: 5, of which 5 were waited for; matrix products, arithmetic and copies ran while one was open for 0% of the time, Pallas kernels for 0%

profile of v1, /device:TPU:1, one launch (start us, length us, event | category | flops | bytes accessed | tf_op | source)
XLA Modules:
  0.0 540.6 jit_solution(6483370212897114953)
XLA Ops:
  6.5 0.0 copy-start
  6.5 0.0 all-reduce.2.cloned.1.call-start
  6.5 0.7 convert_bitcast_fusion
  7.3 0.1 copy.8
  7.4 0.2 mul.32
  7.6 0.4 mul.33
  8.0 0.0 copy-done
  8.0 3.0 fusion.11
  11.1 0.0 all-reduce.2.cloned.1.call-update
  11.1 0.0 all-gather.8.cloned.1.call-start
  11.2 0.7 compare_select_fusion
  11.8 0.7 compare_and_fusion
  12.5 90.8 %all-reduce.2.cloned.1.call-done = f32[512,512]{1,0:T(8,128)} async-done(((f32[512,512]{1,0:T(8,128)}), f32[512,512]{1,0:T(8,128)}) %all-reduce.2.cloned.1.call-update) | async-done | bytes 1048592 | tf_op jit(solution)/shard_map/psum | solution.py:44
  103.3 1.7 sub.38
  105.1 1.6 gather_fusion
  106.7 1.1 fusion.6
  107.9 0.0 all-gather.8.cloned.1.call-update
  107.9 0.2 all-gather.10.cloned.1.call-start
  108.1 94.7 %all-gather.8.cloned.1.call-done = f32[8,512,512]{2,1,0:T(8,128)} async-done(((f32[1,512,512]{2,1,0:T(8,128)}), f32[8,512,512]{2,1,0:T(8,128)}) %all-gather.8.cloned.1.call-update) | async-done | bytes 8388624 | tf_op jit(solution)/shard_map/all_gather | solution.py:14
  202.8 4.5 reduce_sum.36
  207.3 1.9 fusion.2
  209.3 1.9 convolution_subtract_fusion.3
  211.2 1.9 fusion.9
  213.1 1.9 convolution_subtract_fusion.2
  215.0 0.0 copy-start.1
  215.0 1.0 copy-done.1
  216.0 3.2 broadcast_select_fusion.2
  219.2 0.0 all-gather.10.cloned.1.call-update
  219.2 0.3 all-gather.12.cloned.1.call-start
  219.5 93.7 %all-gather.10.cloned.1.call-done = f32[4096,512]{1,0:T(8,128)} async-done(((f32[512,512]{1,0:T(8,128)}), f32[4096,512]{1,0:T(8,128)}) %all-gather.10.cloned.1.call-update) | async-done | bytes 8388624 | tf_op jit(solution)/shard_map/all_gather | solution.py:14
  313.2 5.5 %reduce_sum.37 = f32[512,512]{1,0:T(8,128)} reduce(f32[8,512,512]{2,1,0:T(8,128)} %bitcast.34, f32[]{:T(128)} %constant.130.clone.1), dimensions={0}, to_apply=%region_2.3 | reduce | flops 1835008 | bytes 9437188 | tf_op jit(solution)/shard_map/reduce_sum | solution.py:14
  318.6 5.2 broadcast_select_fusion.1
  323.9 0.0 all-gather.12.cloned.1.call-update
  323.9 0.0 all-gather.14.cloned.1.call-start
  323.9 90.6 %all-gather.12.cloned.1.call-done = f32[4096,512]{1,0:T(8,128)} async-done(((f32[512,512]{1,0:T(8,128)}), f32[4096,512]{1,0:T(8,128)}) %all-gather.12.cloned.1.call-update) | async-done | bytes 8388624 | tf_op jit(solution)/shard_map/all_gather | solution.py:14
  414.5 4.5 reduce_sum.38
  419.0 0.0 copy-start.2
  419.0 1.9 fusion.4
  421.0 1.9 convolution_subtract_fusion.1
  422.9 1.9 fusion.10
  424.8 1.8 convolution_subtract_fusion
  426.7 0.0 copy-done.2
  426.7 3.2 broadcast_select_fusion
  429.8 0.0 all-gather.14.cloned.1.call-update
  429.9 93.9 %all-gather.14.cloned.1.call-done = f32[4096,512]{1,0:T(8,128)} async-done(((f32[512,512]{1,0:T(8,128)}), f32[4096,512]{1,0:T(8,128)}) %all-gather.14.cloned.1.call-update) | async-done | bytes 8388624 | tf_op jit(solution)/shard_map/all_gather | solution.py:14
  523.8 5.5 %reduce_sum.39 = f32[512,512]{1,0:T(8,128)} reduce(f32[8,512,512]{2,1,0:T(8,128)} %bitcast.35, f32[]{:T(128)} %constant.130.clone.1), dimensions={0}, to_apply=%region_4.5 | reduce | flops 1835008 | bytes 9437188 | tf_op jit(solution)/shard_map/reduce_sum | solution.py:14
  529.3 4.8 select_select_fusion
  (5 shorter events, 0.0 us)
Async XLA Ops:
  6.5 1.5 copy-start
  6.5 96.8 %all-reduce.2.cloned.1.call-start = ((), (), s32[]{:S(2)}) async-start(), calls=%async_computation | async-start | bytes 2097152 | tf_op jit(solution)/shard_map/psum | solution.py:44
  11.1 191.7 %all-gather.8.cloned.1.call-start = ((), (), s32[]{:S(2)}) async-start(), calls=%async_computation.1 | async-start | bytes 9437184 | tf_op jit(solution)/shard_map/all_gather | solution.py:14
  107.9 205.3 %all-gather.10.cloned.1.call-start = ((), (), s32[]{:S(2)}) async-start(), calls=%async_computation.2 | async-start | bytes 9437184 | tf_op jit(solution)/shard_map/all_gather | solution.py:14
  215.0 1.0 copy-start.1
  219.2 195.3 %all-gather.12.cloned.1.call-start = ((), (), s32[]{:S(2)}) async-start(), calls=%async_computation.3 | async-start | bytes 9437184 | tf_op jit(solution)/shard_map/all_gather | solution.py:14
  323.9 199.9 %all-gather.14.cloned.1.call-start = ((), (), s32[]{:S(2)}) async-start(), calls=%async_computation.4 | async-start | bytes 9437184 | tf_op jit(solution)/shard_map/all_gather | solution.py:14
  419.0 7.7 %copy-start.2 = (f32[512,512]{1,0:T(8,128)S(1)}, f32[512,512]{1,0:T(8,128)}, u32[]{:S(2)}) copy-start(f32[512,512]{1,0:T(8,128)} %get-tuple-element.48) | copy-start | bytes 3145732
Sparse Core Ops, SparseCore 0:
  11.2 92.0 all-reduce.1
  108.0 94.7 all-gather.7
  219.3 93.7 all-gather.9
  324.0 90.4 all-gather.11
  430.0 93.7 all-gather.13
